TPU v7x, 32 devices: a whole 2x2x4 slice. The times are simulated.
32 devices in a mesh: tp: 2 (over x), ad: 16 (over z, y, core).
Axes of the slice: x: 2, y: 2, z: 4, core: 2. Of those that a mesh axis runs over, the one named last changes fastest.
Arguments:
- tokens: bfloat16 [16384, 8192], P('ad', 'tp'), may hold values from -6 to 6
- value_weight: bfloat16 [8192, 1024], P(('tp', 'ad')), may hold values from -0.0625 to 0.0625
- adapter_down: bfloat16 [32, 8192, 128], P('ad', 'tp'), may hold values from -0.0625 to 0.0625
- adapter_up_panels: bfloat16 [32, 128, 1024], P('ad', None, 'tp'), may hold values from -0.5 to 0.5
- req_start: int32 [16], replicated, may hold values from 0 to 16128, as said below
- req_adapter: int32 [16], replicated, may hold values from 0 to 31
- adapter_home: int32 [32], replicated, may hold values from 0 to 31, each once
Outputs:
- adapted: bfloat16 [16384, 1024], P('ad', 'tp')
Inputs may be any that keep to these rules, and one draw needn't show every extreme that they name: `req_start`: entries rise strictly, the first is 0 and each is a multiple of 256; the tokens of one index of ad meet at most 4 requests, and those of the first index meet exactly 4. Each storage row once; adapter a is stored on index adapter_home[a] // 2 of ad.
All inputs are finite; a program needn't handle non-finite values.
Results may differ from a plain program's by a relative error of at most 0.0085.
Values may be sent and summed in bfloat16 or wider, within the bound.
No kernel may reach another device: no remote copies, remote signals or barrier semaphores. Data moves between devices by JAX's collectives and lax.ppermute only.
A program may use at most 64 MiB of HBM per device.

v0:
```python
import jax
import jax.numpy as jnp
from jax import lax
from jax.sharding import PartitionSpec as P

FMAX = 4
adapter_scale = 2.0


def body(
    tokens, value_weight, adapter_down, adapter_up_panels, req_start, req_adapter, adapter_home
):
    tok_rows = tokens.shape[0]
    width_shard = tokens.shape[1]
    ad_count = lax.axis_size("ad")
    slot_count = FMAX
    block_rows = tok_rows // slot_count
    owned_count = adapter_down.shape[0]
    rank_width = adapter_down.shape[2]
    out_cols = adapter_up_panels.shape[2]
    slab_rows = width_shard // ad_count
    rank_slab = rank_width // ad_count
    total_adapters = owned_count * ad_count
    base_part = jnp.dot(
        tokens,
        lax.all_gather(value_weight, "ad", axis=0, tiled=True),
        preferred_element_type=jnp.float32,
    )
    down_send = adapter_down.reshape(owned_count, ad_count, slab_rows, rank_width)
    up_send = adapter_up_panels.reshape(owned_count, ad_count, rank_slab, out_cols)
    down_slab, up_slab = (
        lax.all_to_all(down_send, "ad", split_axis=1, concat_axis=0, tiled=True),
        lax.all_to_all(up_send, "ad", split_axis=1, concat_axis=0, tiled=True),
    )
    down_slab = down_slab.reshape(total_adapters, slab_rows, rank_width)
    up_slab = up_slab.reshape(total_adapters, rank_slab, out_cols)
    requests = req_start.shape[0]
    req_ids = jnp.arange(requests, dtype=jnp.int32)
    first_rows = jnp.arange(ad_count, dtype=jnp.int32) * tok_rows
    first_req = jnp.sum((req_start[None, :] <= first_rows[:, None]).astype(jnp.int32), axis=1) - 1
    wanted = jnp.minimum(
        first_req[:, None] + jnp.arange(slot_count, dtype=jnp.int32)[None, :], requests - 1
    )
    chosen = jnp.sum(
        jnp.where(wanted[:, :, None] == req_ids[None, None, :], req_adapter[None, None, :], 0),
        axis=2,
    )
    adapter_ids = jnp.arange(total_adapters, dtype=jnp.int32)
    storage = jnp.sum(
        jnp.where(chosen[:, :, None] == adapter_ids[None, None, :], adapter_home[None, None, :], 0),
        axis=2,
    )
    fetch_rows = storage.T
    down_out = jnp.take(down_slab, fetch_rows, axis=0)
    up_out = jnp.take(up_slab, fetch_rows, axis=0)
    down_got, up_got = (
        lax.all_to_all(down_out, "ad", split_axis=1, concat_axis=1, tiled=True),
        lax.all_to_all(up_out, "ad", split_axis=1, concat_axis=1, tiled=True),
    )
    down_got = down_got.reshape(slot_count, width_shard, rank_width)
    up_got = up_got.reshape(slot_count, rank_width, out_cols)
    my_index = lax.axis_index("ad")
    block_first = my_index * tok_rows + jnp.arange(slot_count, dtype=jnp.int32) * block_rows
    block_req = jnp.sum((req_start[None, :] <= block_first[:, None]).astype(jnp.int32), axis=1) - 1
    mine_first = jnp.sum((req_start <= my_index * tok_rows).astype(jnp.int32)) - 1
    block_slot = block_req - mine_first
    block_down = jnp.take(down_got, block_slot, axis=0)
    block_up = jnp.take(up_got, block_slot, axis=0)
    tok_blocks = tokens.reshape(slot_count, block_rows, width_shard)
    rank_part = jnp.einsum(
        "btd,bdr->btr", tok_blocks, block_down, preferred_element_type=jnp.float32
    ).reshape(tok_rows, rank_width)
    rank_full = lax.psum(rank_part, "tp")
    base_value_share = lax.psum_scatter(
        base_part.astype(jnp.bfloat16), "tp", scatter_dimension=1, tiled=True
    ).astype(jnp.float32)
    rank_rounded = rank_full.astype(jnp.bfloat16)
    rank_blocks = rank_rounded.reshape(slot_count, block_rows, rank_width)
    adapter_value_delta = jnp.einsum(
        "btr,brk->btk", rank_blocks, block_up, preferred_element_type=jnp.float32
    ).reshape(tok_rows, out_cols)
    return (base_value_share + adapter_scale * adapter_value_delta).astype(jnp.bfloat16)


def solution(mesh):
    return jax.shard_map(
        body,
        mesh=mesh,
        in_specs=(
            P("ad", "tp"),
            P(("tp", "ad"), None),
            P("ad", "tp", None),
            P("ad", None, "tp"),
            P(),
            P(),
            P(),
        ),
        out_specs=P("ad", "tp"),
        check_vma=False,
    )
```

profile of v0, /device:TPU:12, one launch (start us, length us, event | category | flops | bytes accessed | tf_op | source)
XLA Modules:
  0.0 280.4 jit_solution(1220584968219142080)
XLA Ops:
  6.5 0.0 all-gather.2.cloned.1.call-start
  6.5 0.7 all-gather.2.cloned.1.call-update
  7.3 1.7 copy.40
  8.9 6.2 %all-to-all-start.2 = ((bf16[2,16,8,512]{3,2,0,1:T(8,128)(2,1)}), bf16[2,16,8,512]{3,2,0,1:T(8,128)(2,1)S(1)}, u32[]{:S(2)}, u32[]{:S(2)}) async-start(bf16[2,16,8,512]{3,2,0,1:T(8,128)(2,1)} %copy.40), calls=%async_computation.3 | async-start | bytes 524288 | tf_op jit(solution)/shard_map/all_to_all | solution.py:33
  15.2 0.0 copy-start.2
  15.2 0.0 copy-start
  15.2 0.0 copy-start.1
  15.2 3.2 %copy.34 = bf16[2,16,256,128]{3,2,0,1:T(8,128)(2,1)} copy(bf16[2,16,256,128]{3,2,1,0:T(8,128)(2,1)} %bitcast.43) | data formatting | bytes 4194304 | tf_op jit(solution)/shard_map/reshape | solution.py:29
  18.4 7.5 %all-to-all-done.2 = bf16[2,16,8,512]{3,2,0,1:T(8,128)(2,1)S(1)} async-done(((bf16[2,16,8,512]{3,2,0,1:T(8,128)(2,1)}), bf16[2,16,8,512]{3,2,0,1:T(8,128)(2,1)S(1)}, u32[]{:S(2)}, u32[]{:S(2)}) %all-to-all-start.2) | async-done | bytes 262176 | tf_op jit(solution)/shard_map/all_to_all | solution.py:33
  25.9 8.3 %all-to-all-start = ((bf16[2,16,256,128]{3,2,0,1:T(8,128)(2,1)}), bf16[2,16,256,128]{3,2,0,1:T(8,128)(2,1)S(1)}, u32[]{:S(2)}, u32[]{:S(2)}) async-start(bf16[2,16,256,128]{3,2,0,1:T(8,128)(2,1)} %copy.34), calls=%async_computation.1 | async-start | bytes 4194304 | tf_op jit(solution)/shard_map/all_to_all | solution.py:32
  34.2 0.0 copy-done.2
  34.2 0.2 convert_reduce_fusion
  34.4 0.0 copy-done
  34.4 0.2 select_reduce_fusion.1
  34.7 0.0 copy-done.1
  34.7 0.2 select_reduce_fusion
  34.9 0.1 reshape.113
  35.0 0.1 copy.33
  35.1 0.6 gather_fusion.2
  35.7 0.9 copy_select_fusion.1
  36.6 82.5 %all-to-all-done = bf16[2,16,256,128]{3,2,0,1:T(8,128)(2,1)S(1)} async-done(((bf16[2,16,256,128]{3,2,0,1:T(8,128)(2,1)}), bf16[2,16,256,128]{3,2,0,1:T(8,128)(2,1)S(1)}, u32[]{:S(2)}, u32[]{:S(2)}) %all-to-all-start) | async-done | bytes 2097184 | tf_op jit(solution)/shard_map/all_to_all | solution.py:32
  119.1 4.2 %all-to-all-start.3 = ((bf16[4,16,8,512]{3,2,0,1:T(8,128)(2,1)}), bf16[4,16,8,512]{3,2,0,1:T(8,128)(2,1)S(1)}, u32[]{:S(2)}, u32[]{:S(2)}) async-start(bf16[4,16,8,512]{3,2,0,1:T(8,128)(2,1)} %copy_select_fusion.1), calls=%async_computation.4 | async-start | bytes 1048576 | tf_op jit(solution)/shard_map/all_to_all | solution.py:58
  123.4 3.2 %gather_fusion = bf16[64,256,128]{2,1,0:T(8,128)(2,1)} fusion(bf16[32,256,128]{2,1,0:T(8,128)(2,1)S(1)} %bitcast.39, s32[1024]{0:T(1024)S(1)} %pad_clamp_fusion.1), kind=kCustom, calls=%fused_computation | custom fusion | bytes 8388864 | tf_op jit(solution)/shard_map/jit(_take)/gather | solution.py:54
  126.5 4.6 %copy_select_fusion = bf16[4,16,256,128]{3,2,0,1:T(8,128)(2,1)} fusion(bf16[4,16,256,128]{3,2,1,0:T(8,128)(2,1)} %bitcast.40, pred[4,16]{0,1:T(8,128)(4,1)S(1)} %copy.33), kind=kLoop, calls=%fused_computation.4 | loop fusion | flops 2097152 | bytes 8388672 | tf_op jit(solution)/shard_map/jit(_take)/select_n | solution.py:54
  131.1 5.5 %all-to-all-done.3 = bf16[4,16,8,512]{3,2,0,1:T(8,128)(2,1)S(1)} async-done(((bf16[4,16,8,512]{3,2,0,1:T(8,128)(2,1)}), bf16[4,16,8,512]{3,2,0,1:T(8,128)(2,1)S(1)}, u32[]{:S(2)}, u32[]{:S(2)}) %all-to-all-start.3) | async-done | bytes 524320 | tf_op jit(solution)/shard_map/all_to_all | solution.py:58
  136.7 5.4 %all-to-all-start.1 = ((bf16[4,16,256,128]{3,2,0,1:T(8,128)(2,1)}), bf16[4,16,256,128]{3,2,0,1:T(8,128)(2,1)}, u32[]{:S(2)}, u32[]{:S(2)}) async-start(bf16[4,16,256,128]{3,2,0,1:T(8,128)(2,1)} %copy_select_fusion), calls=%async_computation.2 | async-start | bytes 8388608 | tf_op jit(solution)/shard_map/all_to_all | solution.py:57
  142.1 0.0 reduce-scatter.2.cloned.1.call-start
  142.1 0.0 all-gather.2.cloned.1.call-done
  142.1 14.7 %convolution_convert_fusion = bf16[1024,1024]{1,0:T(8,128)(2,1)} fusion(bf16[1024,4096]{1,0:T(8,128)(2,1)} %param.7, bf16[4096,1024]{1,0:T(8,128)(2,1)} %all-gather.2.cloned.1.call-done), kind=kOutput, calls=%fused_computation.11 | convolution fusion | flops 8590983168 | bytes 18874368 | tf_op jit(solution)/shard_map/dot_general | solution.py:24
  156.8 0.0 reduce-scatter.2.cloned.1.call-update
  156.9 0.6 fusion.11
  158.2 0.2 convert_reduce_fusion.1
  158.4 0.6 gather_fusion.3
  159.0 75.2 %all-to-all-done.1 = bf16[4,16,256,128]{3,2,0,1:T(8,128)(2,1)} async-done(((bf16[4,16,256,128]{3,2,0,1:T(8,128)(2,1)}), bf16[4,16,256,128]{3,2,0,1:T(8,128)(2,1)}, u32[]{:S(2)}, u32[]{:S(2)}) %all-to-all-start.1) | async-done | bytes 4194336 | tf_op jit(solution)/shard_map/all_to_all | solution.py:57
  234.3 4.7 %copy.36 = bf16[4,16,256,128]{3,2,1,0:T(8,128)(2,1)} copy(bf16[4,16,256,128]{3,2,0,1:T(8,128)(2,1)} %all-to-all-done.1) | data formatting | bytes 8388608 | tf_op jit(solution)/shard_map/all_to_all | solution.py:57
  239.0 5.4 %gather_fusion.1 = bf16[4,4096,128]{2,1,0:T(8,128)(2,1)} fusion(bf16[4,4096,128]{2,1,0:T(8,128)(2,1)} %bitcast.41, s32[1024]{0:T(1024)S(1)} %pad_clamp_fusion), kind=kCustom, calls=%fused_computation.1 | custom fusion | bytes 8388624 | tf_op jit(solution)/shard_map/jit(_take)/gather | solution.py:67
  244.3 7.6 %fusion.5 = f32[4,256,128]{1,2,0:T(8,128)S(1)} fusion(bf16[4,256,4096]{2,1,0:T(8,128)(2,1)} %bitcast.49, bf16[4,4096,128]{2,1,0:T(8,128)(2,1)} %gather_fusion.1, pred[4]{0:T(512)(128)(4,1)S(1)} %compare_and_fusion.1), kind=kOutput, calls=%fused_computation.13 | convolution fusion | flops 1075838976 | bytes 13107204 | tf_op jit(solution)/shard_map/btd,bdr->btr/dot_general | solution.py:70
  251.9 0.2 copy.38
  252.1 18.2 %all-reduce.1 = bf16[1024,128]{1,0:T(8,128)(2,1)S(1)} all-reduce(f32[1024,128]{1,0:T(8,128)S(1)} %bitcast.46), channel_id=1, replica_groups=mesh['tp'=2,'ad'=16] {'tp'}, use_global_device_ids=true, to_apply=%region_6.7 | all-reduce | flops 131072 | bytes 786432 | tf_op jit(solution)/shard_map/psum | solution.py:73
  270.3 0.5 convolution_multiply_fusion
  270.8 0.0 reduce-scatter.2.cloned.1.call-done
  270.9 2.7 fusion.3
  (11 shorter events, 0.1 us)
Async XLA Ops:
  6.5 135.6 %all-gather.2.cloned.1.call-start = ((), (), s32[]{:S(2)}) async-start(), calls=%async_computation.5 | async-start | bytes 8912896 | tf_op jit(solution)/shard_map/all_gather | solution.py:26
  8.9 16.9 %all-to-all-start.2 = ((bf16[2,16,8,512]{3,2,0,1:T(8,128)(2,1)}), bf16[2,16,8,512]{3,2,0,1:T(8,128)(2,1)S(1)}, u32[]{:S(2)}, u32[]{:S(2)}) async-start(bf16[2,16,8,512]{3,2,0,1:T(8,128)(2,1)} %copy.40), calls=%async_computation.3 | async-start | bytes 524288 | tf_op jit(solution)/shard_map/all_to_all | solution.py:33
  15.2 19.0 %copy-start.2 = (s32[16]{0:T(128)S(1)}, s32[16]{0:T(128)}, u32[]{:S(2)}) copy-start(s32[16]{0:T(128)} %param.11) | copy-start | bytes 196
  15.2 19.2 %copy-start = (s32[16]{0:T(128)S(1)}, s32[16]{0:T(128)}, u32[]{:S(2)}) copy-start(s32[16]{0:T(128)} %param.12) | copy-start | bytes 196
  15.2 19.5 %copy-start.1 = (s32[32]{0:T(128)S(1)}, s32[32]{0:T(128)}, u32[]{:S(2)}) copy-start(s32[32]{0:T(128)} %param.13) | copy-start | bytes 388
  25.9 93.3 %all-to-all-start = ((bf16[2,16,256,128]{3,2,0,1:T(8,128)(2,1)}), bf16[2,16,256,128]{3,2,0,1:T(8,128)(2,1)S(1)}, u32[]{:S(2)}, u32[]{:S(2)}) async-start(bf16[2,16,256,128]{3,2,0,1:T(8,128)(2,1)} %copy.34), calls=%async_computation.1 | async-start | bytes 4194304 | tf_op jit(solution)/shard_map/all_to_all | solution.py:32
  119.1 17.5 %all-to-all-start.3 = ((bf16[4,16,8,512]{3,2,0,1:T(8,128)(2,1)}), bf16[4,16,8,512]{3,2,0,1:T(8,128)(2,1)S(1)}, u32[]{:S(2)}, u32[]{:S(2)}) async-start(bf16[4,16,8,512]{3,2,0,1:T(8,128)(2,1)} %copy_select_fusion.1), calls=%async_computation.4 | async-start | bytes 1048576 | tf_op jit(solution)/shard_map/all_to_all | solution.py:58
  136.7 97.6 %all-to-all-start.1 = ((bf16[4,16,256,128]{3,2,0,1:T(8,128)(2,1)}), bf16[4,16,256,128]{3,2,0,1:T(8,128)(2,1)}, u32[]{:S(2)}, u32[]{:S(2)}) async-start(bf16[4,16,256,128]{3,2,0,1:T(8,128)(2,1)} %copy_select_fusion), calls=%async_computation.2 | async-start | bytes 8388608 | tf_op jit(solution)/shard_map/all_to_all | solution.py:57
  142.1 128.8 %reduce-scatter.2.cloned.1.call-start = ((), (), s32[]{:S(2)}) async-start(), calls=%async_computation.6 | async-start | bytes 3145728 | tf_op jit(solution)/shard_map/reduce_scatter | solution.py:74
Sparse Core Ops, SparseCore 0:
  9.5 107.7 all-gather.1
  157.0 32.8 reduce-scatter.1
where the time goes:
time: 281 us; the launch traced here: 280 us
  waiting for transfers between devices  172 us (61%)
  starting transfers between devices  24.2 us (9%)
  matrix products  22.8 us (8%)
  local copies, waits for them, and re-layouts  19.7 us (7%)
  blocking collectives  18.2 us (6%)
  between operations  14.2 us (5%)
  other arithmetic  9.73 us (3%)
    all_to_all x1, waiting for transfers between devices, body(): lax.all_to_all(down_send, 'ad', split_axis=1, concat_axis=0, tiled=True)  82.5 us
    all_to_all x1, waiting for transfers between devices, body(): lax.all_to_all(down_out, 'ad', split_axis=1, concat_axis=1, tiled=True)  75.2 us
    psum x1, blocking collectives, body(): rank_full = lax.psum(rank_part, 'tp')  18.2 us
    dot_general x1, matrix products, body(): jnp.dot(tokens, lax.all_gather(value_weight, 'ad', axis=0, tiled=True), p...  14.7 us
    all_to_all x1, starting transfers between devices, body(): lax.all_to_all(down_send, 'ad', split_axis=1, concat_axis=0, tiled=True)  8.33 us
    dot_general x1, matrix products, body(): jnp.einsum('btd,bdr->btr', tok_blocks, block_down, preferred_element_type...  7.56 us
    all_to_all x1, waiting for transfers between devices, body(): lax.all_to_all(up_send, 'ad', split_axis=1, concat_axis=0, tiled=True)  7.49 us
    all_to_all x1, starting transfers between devices, body(): lax.all_to_all(up_send, 'ad', split_axis=1, concat_axis=0, tiled=True)  6.24 us
  transfers between devices with their start and end apart: 6, of which 4 were waited for; matrix products, arithmetic and copies ran while one was open for 18% of the time, Pallas kernels for 0%

commit v1 on v0

--- a/solution.py
+++ b/solution.py
@@ -70,7 +70,8 @@
     rank_part = jnp.einsum(
         "btd,bdr->btr", tok_blocks, block_down, preferred_element_type=jnp.float32
     ).reshape(tok_rows, rank_width)
-    rank_full = lax.psum(rank_part, "tp")
+    shards = lax.all_gather(rank_part, "tp", axis=0, tiled=False)
+    rank_full = shards.sum(axis=0)
     base_value_share = lax.psum_scatter(
         base_part.astype(jnp.bfloat16), "tp", scatter_dimension=1, tiled=True
     ).astype(jnp.float32)

time: 281 us -> 291 us (1.036)
  blocking collectives: 18.2 us -> 31.5 us
  starting transfers between devices: 24.2 us -> 14.8 us
  waiting for transfers between devices: 172 us -> 177 us
    all_to_all x0 -> x2, blocking collectives: none -> 31.5 us  [the longest x1 18.3 us: body(): lax.all_to_all(up_out, 'ad', split_axis=1, concat_axis=1, tiled=True)]
    all_to_all x1, waiting for transfers between devices: 75.2 us -> 95.2 us  [body(): lax.all_to_all(down_out, 'ad', split_axis=1, concat_axis=1, tiled=True)]
    psum x1 -> x0, blocking collectives: 18.2 us -> none  [body(): rank_full = lax.psum(rank_part, 'tp')]
    all_to_all x2 -> x0, waiting for transfers between devices: 13 us -> none  [the longest x1 7.49 us: body(): lax.all_to_all(up_send, 'ad', split_axis=1, concat_axis=0, tiled=True)]
    all_to_all x2 -> x0, starting transfers between devices: 10.5 us -> none  [the longest x1 6.24 us: body(): lax.all_to_all(up_send, 'ad', split_axis=1, concat_axis=0, tiled=True)]
    all_to_all x1, waiting for transfers between devices: 82.5 us -> 74.5 us  [body(): lax.all_to_all(down_send, 'ad', split_axis=1, concat_axis=0, tiled=True)]
    reduce_scatter x1, waiting for transfers between devices: 0.02 us -> 6.18 us  [body(): lax.psum_scatter(base_part.astype(jnp.bfloat16), 'tp', scatter_dimension=...]
    all_to_all x1, starting transfers between devices: 5.4 us -> 8.43 us  [body(): lax.all_to_all(down_out, 'ad', split_axis=1, concat_axis=1, tiled=True)]
  transfers between devices with their start and end apart: 6 -> 5, of which waited for: 4 -> 3; matrix products, arithmetic and copies ran while one was open for 18% -> 17% of each run, Pallas kernels for 0% -> 0%
where the time goes in v1:
time: 291 us; the launch traced here: 288 us
  waiting for transfers between devices  177 us (61%)
  blocking collectives  31.5 us (11%)
  matrix products  22.8 us (8%)
  local copies, waits for them, and re-layouts  18.6 us (6%)
  starting transfers between devices  14.8 us (5%)
  between operations  13.9 us (5%)
  other arithmetic  10.2 us (4%)
    all_to_all x1, waiting for transfers between devices, body(): lax.all_to_all(down_out, 'ad', split_axis=1, concat_axis=1, tiled=True)  95.2 us
    all_to_all x1, waiting for transfers between devices, body(): lax.all_to_all(down_send, 'ad', split_axis=1, concat_axis=0, tiled=True)  74.5 us
    all_to_all x1, blocking collectives, body(): lax.all_to_all(up_out, 'ad', split_axis=1, concat_axis=1, tiled=True)  18.3 us
    dot_general x1, matrix products, body(): jnp.dot(tokens, lax.all_gather(value_weight, 'ad', axis=0, tiled=True), p...  14.7 us
    all_to_all x1, blocking collectives, body(): lax.all_to_all(up_send, 'ad', split_axis=1, concat_axis=0, tiled=True)  13.2 us
    all_to_all x1, starting transfers between devices, body(): lax.all_to_all(down_out, 'ad', split_axis=1, concat_axis=1, tiled=True)  8.43 us
    dot_general x1, matrix products, body(): jnp.einsum('btd,bdr->btr', tok_blocks, block_down, preferred_element_type...  7.56 us
    all_to_all x1, starting transfers between devices, body(): lax.all_to_all(down_send, 'ad', split_axis=1, concat_axis=0, tiled=True)  6.24 us
  transfers between devices with their start and end apart: 5, of which 3 were waited for; matrix products, arithmetic and copies ran while one was open for 17% of the time, Pallas kernels for 0%

profile of v1, /device:TPU:12, one launch (start us, length us, event | category | flops | bytes accessed | tf_op | source)
XLA Modules:
  0.0 288.4 jit_solution(7821127958498643764)
XLA Ops:
  6.5 0.0 all-gather.3.cloned.1.call-start
  6.5 0.7 all-gather.3.cloned.1.call-update
  7.3 0.0 copy-start.3
  7.3 0.0 copy-start.1
  7.3 0.0 copy-start.2
  7.3 3.2 %copy.34 = bf16[2,16,256,128]{3,2,0,1:T(8,128)(2,1)} copy(bf16[2,16,256,128]{3,2,1,0:T(8,128)(2,1)} %bitcast.43) | data formatting | bytes 4194304 | tf_op jit(solution)/shard_map/reshape | solution.py:29
  10.5 6.2 %all-to-all-start = ((bf16[2,16,256,128]{3,2,0,1:T(8,128)(2,1)}), bf16[2,16,256,128]{3,2,0,1:T(8,128)(2,1)S(1)}, u32[]{:S(2)}, u32[]{:S(2)}) async-start(bf16[2,16,256,128]{3,2,0,1:T(8,128)(2,1)} %copy.34), calls=%async_computation.1 | async-start | bytes 4194304 | tf_op jit(solution)/shard_map/all_to_all | solution.py:32
  16.8 0.0 copy-done.3
  16.8 0.2 convert_reduce_fusion
  17.0 0.0 copy-done.1
  17.0 0.2 select_reduce_fusion.1
  17.2 0.0 copy-done.2
  17.2 0.2 select_reduce_fusion
  17.4 0.1 reshape.108
  17.5 0.1 copy.33
  17.6 74.5 %all-to-all-done = bf16[2,16,256,128]{3,2,0,1:T(8,128)(2,1)S(1)} async-done(((bf16[2,16,256,128]{3,2,0,1:T(8,128)(2,1)}), bf16[2,16,256,128]{3,2,0,1:T(8,128)(2,1)S(1)}, u32[]{:S(2)}, u32[]{:S(2)}) %all-to-all-start) | async-done | bytes 2097184 | tf_op jit(solution)/shard_map/all_to_all | solution.py:32
  92.2 3.1 %gather_fusion = bf16[64,256,128]{2,1,0:T(8,128)(2,1)} fusion(bf16[32,256,128]{2,1,0:T(8,128)(2,1)S(1)} %bitcast.39, s32[1024]{0:T(1024)S(1)} %pad_clamp_fusion.1), kind=kCustom, calls=%fused_computation | custom fusion | bytes 8388864 | tf_op jit(solution)/shard_map/jit(_take)/gather | solution.py:54
  95.2 4.6 %copy_select_fusion = bf16[4,16,256,128]{3,2,0,1:T(8,128)(2,1)} fusion(bf16[4,16,256,128]{3,2,1,0:T(8,128)(2,1)} %bitcast.40, pred[4,16]{0,1:T(8,128)(4,1)S(1)} %copy.33), kind=kLoop, calls=%fused_computation.4 | loop fusion | flops 2097152 | bytes 8388672 | tf_op jit(solution)/shard_map/jit(_take)/select_n | solution.py:54
  99.8 8.4 %all-to-all-start.1 = ((bf16[4,16,256,128]{3,2,0,1:T(8,128)(2,1)}), bf16[4,16,256,128]{3,2,0,1:T(8,128)(2,1)}, u32[]{:S(2)}, u32[]{:S(2)}) async-start(bf16[4,16,256,128]{3,2,0,1:T(8,128)(2,1)} %copy_select_fusion), calls=%async_computation.2 | async-start | bytes 8388608 | tf_op jit(solution)/shard_map/all_to_all | solution.py:57
  108.2 0.0 all-gather.5.cloned.1.call-start
  108.3 0.6 fusion.11
  109.6 0.2 convert_reduce_fusion.1
  109.8 95.2 %all-to-all-done.1 = bf16[4,16,256,128]{3,2,0,1:T(8,128)(2,1)} async-done(((bf16[4,16,256,128]{3,2,0,1:T(8,128)(2,1)}), bf16[4,16,256,128]{3,2,0,1:T(8,128)(2,1)}, u32[]{:S(2)}, u32[]{:S(2)}) %all-to-all-start.1) | async-done | bytes 4194336 | tf_op jit(solution)/shard_map/all_to_all | solution.py:57
  205.0 4.6 %copy.36 = bf16[4,16,256,128]{3,2,1,0:T(8,128)(2,1)} copy(bf16[4,16,256,128]{3,2,0,1:T(8,128)(2,1)} %all-to-all-done.1) | data formatting | bytes 8388608 | tf_op jit(solution)/shard_map/all_to_all | solution.py:57
  209.6 5.2 %gather_fusion.1 = bf16[4,4096,128]{2,1,0:T(8,128)(2,1)} fusion(bf16[4,4096,128]{2,1,0:T(8,128)(2,1)} %bitcast.41, s32[1024]{0:T(1024)S(1)} %pad_clamp_fusion), kind=kCustom, calls=%fused_computation.1 | custom fusion | bytes 8388624 | tf_op jit(solution)/shard_map/jit(_take)/gather | solution.py:67
  214.9 7.6 %fusion.5 = f32[4,256,128]{1,2,0:T(8,128)S(1)} fusion(bf16[4,256,4096]{2,1,0:T(8,128)(2,1)} %bitcast.49, bf16[4,4096,128]{2,1,0:T(8,128)(2,1)} %gather_fusion.1, pred[4]{0:T(512)(128)(4,1)S(1)} %compare_and_fusion.1), kind=kOutput, calls=%fused_computation.13 | convolution fusion | flops 1075838976 | bytes 13107204 | tf_op jit(solution)/shard_map/btd,bdr->btr/dot_general | solution.py:70
  222.5 1.0 copy.38
  223.5 0.0 all-gather.5.cloned.1.call-update
  223.5 0.0 copy-start
  223.5 0.0 reduce-scatter.2.cloned.1.call-start
  223.5 0.0 all-gather.3.cloned.1.call-done
  223.6 14.7 %convolution_convert_fusion = bf16[1024,1024]{1,0:T(8,128)(2,1)} fusion(bf16[1024,4096]{1,0:T(8,128)(2,1)} %param.7, bf16[4096,1024]{1,0:T(8,128)(2,1)} %all-gather.3.cloned.1.call-done), kind=kOutput, calls=%fused_computation.11 | convolution fusion | flops 8590983168 | bytes 18874368 | tf_op jit(solution)/shard_map/dot_general | solution.py:24
  238.3 0.0 reduce-scatter.2.cloned.1.call-update
  238.3 0.0 copy-done
  238.3 13.2 %all_to_all.40 = bf16[2,16,8,512]{3,2,0,1:T(8,128)(2,1)S(1)} all-to-all(bf16[2,16,8,512]{3,2,0,1:T(8,128)(2,1)S(1)} %copy.40), channel_id=1, replica_groups=mesh['tp'=2,'ad'=16] {'ad'}, dimensions={1} | all-to-all | bytes 524288 | tf_op jit(solution)/shard_map/all_to_all | solution.py:33
  251.5 0.6 gather_fusion.2
  252.1 0.1 copy_select_fusion.1
  252.2 18.3 %all_to_all.41 = bf16[4,16,8,512]{3,2,0,1:T(8,128)(2,1)S(1)} all-to-all(bf16[4,16,8,512]{3,2,0,1:T(8,128)(2,1)S(1)} %copy_select_fusion.1), channel_id=1, replica_groups=mesh['tp'=2,'ad'=16] {'ad'}, dimensions={1} | all-to-all | bytes 1048576 | tf_op jit(solution)/shard_map/all_to_all | solution.py:58
  270.6 0.6 gather_fusion.3
  271.2 0.0 all-gather.5.cloned.1.call-done
  271.2 1.3 reduce_sum.59
  272.5 0.5 convolution_multiply_fusion
  273.0 6.2 %reduce-scatter.2.cloned.1.call-done = bf16[1024,512]{1,0:T(8,128)(2,1)} async-done(((bf16[1024,1024]{1,0:T(8,128)(2,1)}), bf16[1024,512]{1,0:T(8,128)(2,1)}) %reduce-scatter.2.cloned.1.call-update) | async-done | bytes 1048592 | tf_op jit(solution)/shard_map/reduce_scatter | solution.py:75
  279.2 2.7 fusion.3
  (12 shorter events, 0.1 us)
Async XLA Ops:
  6.5 217.0 %all-gather.3.cloned.1.call-start = ((), (), s32[]{:S(2)}) async-start(), calls=%async_computation.5 | async-start | bytes 8912896 | tf_op jit(solution)/shard_map/all_gather | solution.py:26
  7.3 9.5 %copy-start.3 = (s32[16]{0:T(128)S(1)}, s32[16]{0:T(128)}, u32[]{:S(2)}) copy-start(s32[16]{0:T(128)} %param.11) | copy-start | bytes 196
  7.3 9.7 %copy-start.1 = (s32[16]{0:T(128)S(1)}, s32[16]{0:T(128)}, u32[]{:S(2)}) copy-start(s32[16]{0:T(128)} %param.12) | copy-start | bytes 196
  7.3 9.9 %copy-start.2 = (s32[32]{0:T(128)S(1)}, s32[32]{0:T(128)}, u32[]{:S(2)}) copy-start(s32[32]{0:T(128)} %param.13) | copy-start | bytes 388
  10.5 81.6 %all-to-all-start = ((bf16[2,16,256,128]{3,2,0,1:T(8,128)(2,1)}), bf16[2,16,256,128]{3,2,0,1:T(8,128)(2,1)S(1)}, u32[]{:S(2)}, u32[]{:S(2)}) async-start(bf16[2,16,256,128]{3,2,0,1:T(8,128)(2,1)} %copy.34), calls=%async_computation.1 | async-start | bytes 4194304 | tf_op jit(solution)/shard_map/all_to_all | solution.py:32
  99.8 105.2 %all-to-all-start.1 = ((bf16[4,16,256,128]{3,2,0,1:T(8,128)(2,1)}), bf16[4,16,256,128]{3,2,0,1:T(8,128)(2,1)}, u32[]{:S(2)}, u32[]{:S(2)}) async-start(bf16[4,16,256,128]{3,2,0,1:T(8,128)(2,1)} %copy_select_fusion), calls=%async_computation.2 | async-start | bytes 8388608 | tf_op jit(solution)/shard_map/all_to_all | solution.py:57
  108.2 163.0 %all-gather.5.cloned.1.call-start = ((), (), s32[]{:S(2)}) async-start(), calls=%async_computation.7 | async-start | bytes 1572864 | tf_op jit(solution)/shard_map/all_gather | solution.py:73
  223.5 14.8 %copy-start = (bf16[2,128,512]{2,1,0:T(8,128)(2,1)S(1)}, bf16[2,128,512]{2,1,0:T(8,128)(2,1)}, u32[]{:S(2)}) copy-start(bf16[2,128,512]{2,1,0:T(8,128)(2,1)} %param.10) | copy-start | bytes 786436
  223.5 55.7 %reduce-scatter.2.cloned.1.call-start = ((), (), s32[]{:S(2)}) async-start(), calls=%async_computation.6 | async-start | bytes 3145728 | tf_op jit(solution)/shard_map/reduce_scatter | solution.py:75
Sparse Core Ops, SparseCore 0:
  9.5 113.9 all-gather.2
  223.6 21.3 all-gather.4
  247.2 31.8 reduce-scatter.1
